TPU v7x, 128 devices: a whole 4x4x4 slice. The times are simulated.
128 devices in a mesh: vrow: 8 (over z, y_hi), img: 16 (over x, y_lo, core).
Axes of the slice: x: 4, y: 4 (y_hi: 2, y_lo: 2; y = y_hi * 2 + y_lo), z: 4, core: 2. Of those that a mesh axis runs over, the one named last changes fastest.
Arguments:
- features: bfloat16 [8, 16, 128, 1024], P('vrow', None, 'img'), may hold values from -6 to 6
- weight_h: bfloat16 [64, 64, 3, 3], replicated, may hold values from -0.25 to 0.25
- weight_v: bfloat16 [64, 64, 3, 3], replicated, may hold values from -0.25 to 0.25
- beta_h: float32 [5, 64], replicated, may hold values from 0.2 to 1
- beta_v: float32 [5, 64], replicated, may hold values from 0.2 to 1
- shear_set: int32 [5], replicated, may hold values from -2 to 2
- cotangent: bfloat16 [16, 128, 8192], P('vrow', 'img'), may hold values from -6 to 6
Outputs:
- output: bfloat16 [16, 128, 8192], P('vrow', 'img')
- grad_features: bfloat16 [8, 16, 128, 1024], P('vrow', None, 'img')
- grad_weight_h: float32 [64, 64, 3, 3], replicated
- grad_weight_v: float32 [64, 64, 3, 3], replicated
- grad_beta_h: float32 [5, 64], replicated
- grad_beta_v: float32 [5, 64], replicated
All inputs are finite; a program needn't handle non-finite values.
Results may differ from a plain program's by a relative error of at most 0.0057.
Values may be sent and summed in bfloat16 or wider, within the bound.
No kernel may reach another device: no remote copies, remote signals or barrier semaphores. Data moves between devices by JAX's collectives and lax.ppermute only.
A program may use at most 128 MiB of HBM per device.

v0:
```python
import jax
import jax.numpy as jnp
from jax import lax
from jax.sharding import PartitionSpec as P

SHIFT_MAX = 2


def conv_taps(source, kernel_row):
    return lax.conv_general_dilated(
        source,
        kernel_row,
        (1, 1),
        ((0, 0), (0, 0)),
        dimension_numbers=("NCHW", "OIHW", "NCHW"),
        preferred_element_type=jnp.float32,
    )


def conv_back(grads, kernel_row):
    return lax.conv_general_dilated(
        grads,
        kernel_row,
        (1, 1),
        ((0, 0), (0, 0)),
        dimension_numbers=("NCHW", "IOHW", "NCHW"),
        preferred_element_type=jnp.float32,
    )


def conv_weight(grads, source):
    result = lax.conv_general_dilated(
        source,
        grads,
        (1, 1),
        ((0, 0), (0, 0)),
        dimension_numbers=("CNHW", "IOHW", "NCHW"),
        preferred_element_type=jnp.float32,
    )
    return jnp.transpose(result, (1, 0, 2, 3))


def view_offsets(count):
    return jnp.arange(count, dtype=jnp.int32) - count // 2


def pad_views(field):
    return jnp.pad(field, ((0, 0), (0, 0), (1, 1), (0, 0)))


def window(padded, row_start, col_start, width):
    starts = (jnp.int32(0), jnp.int32(0), jnp.int32(row_start), jnp.asarray(col_start))
    sizes = (padded.shape[0], padded.shape[1], padded.shape[2] - 2, width + 2)
    return lax.dynamic_slice(padded, starts, sizes)


def masked_source(extended, amounts, start, total):
    columns = start + jnp.arange(extended.shape[3], dtype=jnp.int32)
    shifted = columns[None, :] - amounts[:, None]
    inside = (shifted >= 0) & (shifted < total)
    return (extended * inside[None, None].astype(extended.dtype), inside)


def forward_pass(extended, kernel, blend, shear_set, start, total, reach):
    width = extended.shape[3] - 2 * reach
    offsets = view_offsets(extended.shape[2])
    source_local = extended[:, :, :, reach : reach + width]
    branch = jnp.zeros(source_local.shape, jnp.float32)
    saved = []
    for shear_idx in range(shear_set.shape[0]):
        disparity = shear_set[shear_idx]
        amounts = disparity * offsets
        masked, inside = masked_source(extended, amounts, start, total)
        masked_pad = pad_views(masked)
        preact = jnp.zeros(source_local.shape, jnp.float32)
        for tap_row in range(3):
            piece = window(masked_pad, tap_row, reach - 1 + (tap_row - 1) * disparity, width)
            preact = preact + conv_taps(piece, kernel[:, :, tap_row : tap_row + 1, :])
        keep = inside[:, reach : reach + width].astype(jnp.float32)[None, None]
        branch = branch + blend[shear_idx][None, :, None, None] * (keep * jax.nn.silu(preact))
        saved.append((masked_pad, preact, keep, disparity))
    return ((source_local.astype(jnp.float32) + branch).astype(jnp.bfloat16), saved)


def backward_pass(kernel, blend, grads, saved, extend, reach):
    width = grads.shape[3]
    channels = kernel.shape[0]
    kernel_grad = jnp.zeros((channels, channels, 3, 3), jnp.float32)
    blend_rows = []
    dpre_list = []
    for shear_idx in range(len(saved)):
        masked_pad, preact, keep, disparity = saved[shear_idx]
        blend_rows.append(jnp.sum(grads * (keep * jax.nn.silu(preact)), axis=(0, 2, 3)))
        sigma = jax.nn.sigmoid(preact)
        slope = sigma * (1.0 + preact * (1.0 - sigma))
        dpre = (blend[shear_idx][None, :, None, None] * grads * slope * keep).astype(jnp.bfloat16)
        dpre_list.append(dpre)
        pieces = []
        for tap_row in range(3):
            piece = window(masked_pad, tap_row, reach - 1 + (tap_row - 1) * disparity, width)
            pieces.append(conv_weight(dpre, piece))
        kernel_grad = kernel_grad + jnp.concatenate(pieces, axis=2)
    stacked = extend(jnp.stack(dpre_list))
    total = grads
    for shear_idx in range(len(saved)):
        masked_pad, preact, keep, disparity = saved[shear_idx]
        dpre_pad = pad_views(stacked[shear_idx])
        inputs_grad = jnp.zeros(grads.shape, jnp.float32)
        for tap_row in range(3):
            piece = window(dpre_pad, 2 - tap_row, reach - 1 - (tap_row - 1) * disparity, width)
            inputs_grad = inputs_grad + conv_back(piece, kernel[:, :, tap_row : tap_row + 1, ::-1])
        total = total + keep * inputs_grad
    return (total.astype(jnp.bfloat16), kernel_grad, jnp.stack(blend_rows))


def per_device(features, weight_h, weight_v, beta_h, beta_v, shear_set, cotangent):
    reach = SHIFT_MAX + 1
    vrow_count = lax.axis_size("vrow")
    img_count = lax.axis_size("img")
    channels = weight_h.shape[0]
    u_local, y_all, x_local, merged = features.shape
    v_all = merged // channels
    v_local = v_all // vrow_count
    u_all = u_local * vrow_count
    x_all = x_local * img_count
    y_local = y_all // img_count

    def zero_rims(field):
        widths = [(0, 0)] * (field.ndim - 1) + [(reach, reach)]
        return jnp.pad(field, widths)

    lines = lax.all_to_all(features, "img", split_axis=1, concat_axis=2, tiled=True)
    layout = jnp.transpose(
        lines.reshape(u_local, y_local, x_all, v_all, channels), (0, 1, 4, 3, 2)
    ).reshape(u_local * y_local, channels, v_all, x_all)
    extended_h = zero_rims(layout)
    start_h = -reach
    hfeat, saved_h = forward_pass(extended_h, weight_h, beta_h, shear_set, start_h, x_all, reach)
    block = hfeat.reshape(u_local, y_local, channels, v_all, x_all)
    moved = lax.all_to_all(
        lax.all_to_all(block, "vrow", split_axis=3, concat_axis=0, tiled=True),
        "img",
        split_axis=4,
        concat_axis=1,
        tiled=True,
    )
    vert_in = jnp.transpose(moved, (3, 4, 2, 0, 1)).reshape(
        v_local * x_local, channels, u_all, y_all
    )
    vout, saved_v = forward_pass(
        zero_rims(vert_in), weight_v, beta_v, shear_set, -reach, y_all, reach
    )
    output = jnp.transpose(
        vout.reshape(v_local, x_local, channels, u_all, y_all), (0, 1, 3, 4, 2)
    ).reshape(v_local, x_local, u_all * y_all * channels)
    grad_v = (
        jnp.transpose(cotangent.reshape(v_local, x_local, u_all, y_all, channels), (0, 1, 4, 2, 3))
        .reshape(v_local * x_local, channels, u_all, y_all)
        .astype(jnp.float32)
    )
    dvert, raw_weight_v, raw_beta_v = backward_pass(
        weight_v, beta_v, grad_v, saved_v, zero_rims, reach
    )
    back_block = jnp.transpose(
        dvert.reshape(v_local, x_local, channels, u_all, y_all), (3, 4, 2, 0, 1)
    )
    returned = lax.all_to_all(
        lax.all_to_all(back_block, "vrow", split_axis=0, concat_axis=3, tiled=True),
        "img",
        split_axis=1,
        concat_axis=4,
        tiled=True,
    )
    grad_h = returned.reshape(u_local * y_local, channels, v_all, x_all)
    dhor, raw_weight_h, raw_beta_h = backward_pass(
        weight_h, beta_h, grad_h.astype(jnp.float32), saved_h, zero_rims, reach
    )
    dhor_stored = jnp.transpose(
        dhor.reshape(u_local, y_local, channels, v_all, x_all), (0, 1, 4, 3, 2)
    ).reshape(u_local, y_local, x_all, v_all * channels)
    grad_features = lax.all_to_all(dhor_stored, "img", split_axis=2, concat_axis=1, tiled=True)
    raw_weight_h, raw_weight_v, raw_beta_h, raw_beta_v = lax.psum(
        (raw_weight_h, raw_weight_v, raw_beta_h, raw_beta_v), ("vrow", "img")
    )
    factor = float(u_all * v_all * y_all * x_all) ** (-0.5)
    return (
        output,
        grad_features,
        raw_weight_h * factor,
        raw_weight_v * factor,
        raw_beta_h * factor,
        raw_beta_v * factor,
    )


def solution(mesh):
    placed = (P("vrow", None, "img", None), P(), P(), P(), P(), P(), P("vrow", "img", None))
    return jax.shard_map(
        per_device,
        mesh=mesh,
        in_specs=placed,
        out_specs=(P("vrow", "img", None), P("vrow", None, "img", None), P(), P(), P(), P()),
        check_vma=False,
    )
```

profile of v0, /device:TPU:1, one launch (start us, length us, event | category | flops | bytes accessed | tf_op | source)
XLA Modules:
  0.0 720.8 jit_solution(4382883863679388415)
XLA Ops:
  7.2 6.8 all-to-all-start
  38.2 15.4 %broadcast_multiply_fusion.4 = (bf16[1,64,16,134]{1,0,3,2:T(2,128)(2,1)S(1)}, bf16[1,64,16,134]{1,0,3,2:T(2,128)(2,1)S(1)}, bf16[1,64,16,134]{1,0,3,2:T(2,128)(2...) fusion(bf16[16,134]{1,0:T(8,128)(2,1)S(1)} %copy-done.121, bf16[1,64,16,128]{1,0,3,2:T(2,128)(2,1)S(1)} %copy.364, ...), kind=kLoop, calls=%fused_computation.390 | loop fusion | flops 686080 | bytes 1655744 | tf_op jit(solution)/shard_map/mul | solution.py:61
  132.4 6.5 pad_dynamic-slice_fusion.35
  166.7 6.9 pad_dynamic-slice_fusion.31
  216.6 7.4 %all-to-all-start.1 = ((bf16[1,1,64,16,128]{4,2,1,0,3:T(8,128)(2,1)}), bf16[1,1,64,16,128]{4,2,1,0,3:T(8,128)(2,1)S(1)}, u32[]{:S(2)}, u32[]{:S(2)}) async-start(bf16[1,1,64,16,128]{4,2,1,0,3:T(8,128)(2,1)} %copy.435), calls=%async_computation.1 | async-start | bytes 524288 | tf_op jit(solution)/shard_map/all_to_all | solution.py:141
  224.7 7.8 %all-to-all-done.1 = bf16[1,1,64,16,128]{4,2,1,0,3:T(8,128)(2,1)S(1)} async-done(((bf16[1,1,64,16,128]{4,2,1,0,3:T(8,128)(2,1)}), bf16[1,1,64,16,128]{4,2,1,0,3:T(8,128)(2,1)S(1)}, u32[]{:S(2)}, u32[]{:S(2)}) %all-to-all-start.1) | async-done | bytes 262176 | tf_op jit(solution)/shard_map/all_to_all | solution.py:141
  234.4 6.1 all-to-all-start.2
  321.2 5.7 fusion.86
  332.5 6.3 all-to-all-start.4
  353.9 4.3 fusion.665
  358.2 4.5 fusion.666
  362.7 4.5 fusion.664
  372.8 4.5 fusion.663
  377.4 4.5 fusion.661
  383.1 4.3 fusion.659
  387.5 4.5 fusion.660
  392.0 4.5 fusion.658
  397.8 4.3 fusion.656
  406.0 4.5 fusion.655
  411.8 4.3 fusion.653
  416.1 4.5 fusion.654
  420.7 4.5 fusion.652
  485.4 63.5 %all-reduce.24 = (f32[5,64]{1,0:T(8,128)S(1)}, f32[5,64]{1,0:T(8,128)S(1)}) all-reduce(f32[5,64]{1,0:T(8,128)S(1)} %stack.89, f32[5,64]{1,0:T(8,128)S(1)} %copy-done.126), channel_id=1, replica_groups=mesh['vrow'=8,'img'=16] {'vrow','img'}, use_global_device_ids=true, to_apply=%region_7.8 | all-reduce | flops 640 | bytes 5120 | tf_op jit(solution)/shard_map/psum | solution.py:182
  559.4 150.5 %all-reduce.28.cloned.1.call-done = (f32[64,64,3,3]{0,1,3,2:T(8,128)}, f32[64,64,3,3]{0,1,3,2:T(8,128)}) async-done(((f32[64,64,3,3]{0,1,3,2:T(8,128)}, f32[64,64,3,3]{0,1,3,2:T(8,128)}), (f32[64,64,3,3]{0,1,3,2:T(8,128)}, f32[64,64,3,3]{0,1,3,2:T(8,128)})) %all-reduce.28.cloned.1.call-update) | async-done | bytes 294928 | tf_op jit(solution)/shard_map/psum | solution.py:182
  (669 shorter events, 340.5 us)
Async XLA Ops:
  7.2 29.0 %all-to-all-start = ((bf16[1,16,8,1024]{3,2,0,1:T(8,128)(2,1)}), bf16[1,16,8,1024]{3,2,0,1:T(8,128)(2,1)S(1)}, u32[]{:S(2)}, u32[]{:S(2)}) async-start(bf16[1,16,8,1024]{3,2,0,1:T(8,128)(2,1)} %bitcast.649), calls=%async_computation | async-start | bytes 524288 | tf_op jit(solution)/shard_map/all_to_all | solution.py:132
  53.6 56.2 %copy-start.3 = (bf16[1,64,16,134]{1,0,3,2:T(2,128)(2,1)}, bf16[1,64,16,134]{1,0,3,2:T(2,128)(2,1)S(1)}, u32[]{:S(2)}) copy-start(bf16[1,64,16,134]{1,0,3,2:T(2,128)(2,1)S(1)} %get-tuple-element.100) | copy-start | bytes 823300
  53.6 78.7 %copy-start.5 = (bf16[1,64,16,134]{1,0,3,2:T(2,128)(2,1)}, bf16[1,64,16,134]{1,0,3,2:T(2,128)(2,1)S(1)}, u32[]{:S(2)}) copy-start(bf16[1,64,16,134]{1,0,3,2:T(2,128)(2,1)S(1)} %get-tuple-element.101) | copy-start | bytes 823300
  53.6 78.7 %copy-start.7 = (bf16[1,64,16,134]{1,0,3,2:T(2,128)(2,1)}, bf16[1,64,16,134]{1,0,3,2:T(2,128)(2,1)S(1)}, u32[]{:S(2)}) copy-start(bf16[1,64,16,134]{1,0,3,2:T(2,128)(2,1)S(1)} %get-tuple-element.102) | copy-start | bytes 823300
  132.3 81.9 %copy-start.12 = (f32[16,1,128,64]{2,0,3,1:T(8,128)}, f32[16,1,128,64]{2,0,3,1:T(8,128)S(1)}, u32[]{:S(2)}) copy-start(f32[16,1,128,64]{2,0,3,1:T(8,128)S(1)} %copy.541) | copy-start | bytes 1572868
  159.0 55.2 %copy-start.14 = (f32[16,1,128,64]{2,0,3,1:T(8,128)}, f32[16,1,128,64]{2,0,3,1:T(8,128)S(1)}, u32[]{:S(2)}) copy-start(f32[16,1,128,64]{2,0,3,1:T(8,128)S(1)} %copy.542) | copy-start | bytes 1572868
  206.4 7.8 %copy-start.18 = (f32[16,1,128,64]{2,0,3,1:T(8,128)}, f32[16,1,128,64]{2,0,3,1:T(8,128)S(1)}, u32[]{:S(2)}) copy-start(f32[16,1,128,64]{2,0,3,1:T(8,128)S(1)} %copy.544) | copy-start | bytes 1572868
  214.3 9.6 %copy-start.153 = (f32[5,64]{1,0:T(8,128)S(1)}, f32[5,64]{1,0:T(8,128)}, u32[]{:S(2)}) copy-start(f32[5,64]{1,0:T(8,128)} %param.11) | copy-start | bytes 3844
  214.3 10.2 %copy-start.140 = (pred[8,22]{1,0:T(8,128)(4,1)S(1)}, pred[8,22]{1,0:T(8,128)(4,1)}, u32[]{:S(2)}) copy-start(pred[8,22]{1,0:T(8,128)(4,1)} %get-tuple-element.141) | copy-start | bytes 532
  214.4 10.2 %copy-start.141 = (pred[8,22]{1,0:T(8,128)(4,1)S(1)}, pred[8,22]{1,0:T(8,128)(4,1)}, u32[]{:S(2)}) copy-start(pred[8,22]{1,0:T(8,128)(4,1)} %get-tuple-element.164) | copy-start | bytes 532
  216.6 15.9 %all-to-all-start.1 = ((bf16[1,1,64,16,128]{4,2,1,0,3:T(8,128)(2,1)}), bf16[1,1,64,16,128]{4,2,1,0,3:T(8,128)(2,1)S(1)}, u32[]{:S(2)}, u32[]{:S(2)}) async-start(bf16[1,1,64,16,128]{4,2,1,0,3:T(8,128)(2,1)} %copy.435), calls=%async_computation.1 | async-start | bytes 524288 | tf_op jit(solution)/shard_map/all_to_all | solution.py:141
  224.6 47.6 %copy-start.142 = (f32[64]{0:T(128)}, f32[64]{0:T(128)S(1)}, u32[]{:S(2)}) copy-start(f32[64]{0:T(128)S(1)} %get-tuple-element.126) | copy-start | bytes 772
  234.4 20.1 %copy-start.137 = (pred[8,22]{1,0:T(8,128)(4,1)S(1)}, pred[8,22]{1,0:T(8,128)(4,1)}, u32[]{:S(2)}) copy-start(pred[8,22]{1,0:T(8,128)(4,1)} %get-tuple-element.160) | copy-start | bytes 532
  234.4 20.1 %copy-start.138 = (pred[8,22]{1,0:T(8,128)(4,1)S(1)}, pred[8,22]{1,0:T(8,128)(4,1)}, u32[]{:S(2)}) copy-start(pred[8,22]{1,0:T(8,128)(4,1)} %get-tuple-element.162) | copy-start | bytes 532
  234.4 20.2 %copy-start.50 = (f32[16,8,17,64]{3,1,2,0:T(8,128)S(1)}, f32[16,8,17,64]{3,1,2,0:T(8,128)}, u32[]{:S(2)}) copy-start(f32[16,8,17,64]{3,1,2,0:T(8,128)} %get-tuple-element.88) | copy-start | bytes 1671172
  234.4 33.3 %all-to-all-start.2 = ((bf16[16,2,4096]{2,1,0:T(2,128)(2,1)}), bf16[16,2,4096]{2,1,0:T(2,128)(2,1)}, u32[]{:S(2)}, u32[]{:S(2)}) async-start(bf16[16,2,4096]{2,1,0:T(2,128)(2,1)} %reshape.837), calls=%async_computation.2 | async-start | bytes 524288 | tf_op jit(solution)/shard_map/all_to_all | solution.py:140
  317.1 12.8 %all-to-all-start.3 = ((bf16[8,2,8192]{2,1,0:T(2,128)(2,1)}), bf16[8,2,8192]{2,1,0:T(2,128)(2,1)}, u32[]{:S(2)}, u32[]{:S(2)}) async-start(bf16[8,2,8192]{2,1,0:T(2,128)(2,1)} %reshape.839), calls=%async_computation.3 | async-start | bytes 524288 | tf_op jit(solution)/shard_map/all_to_all | solution.py:168
  332.5 13.7 %all-to-all-start.4 = ((bf16[16,2,4096]{2,1,0:T(2,128)(2,1)}), bf16[16,2,4096]{2,1,0:T(2,128)(2,1)S(1)}, u32[]{:S(2)}, u32[]{:S(2)}) async-start(bf16[16,2,4096]{2,1,0:T(2,128)(2,1)} %reshape.841), calls=%async_computation.4 | async-start | bytes 524288 | tf_op jit(solution)/shard_map/all_to_all | solution.py:167
  550.1 7.7 %copy-start.79 = (f32[64,64,1,3]{0,1,3,2:T(8,128)S(1)}, f32[64,64,1,3]{0,1,3,2:T(8,128)}, u32[]{:S(2)}) copy-start(f32[64,64,1,3]{0,1,3,2:T(8,128)} %fusion.665) | copy-start | bytes 147460
  550.1 7.7 %copy-start.80 = (f32[64,64,1,3]{0,1,3,2:T(8,128)S(1)}, f32[64,64,1,3]{0,1,3,2:T(8,128)}, u32[]{:S(2)}) copy-start(f32[64,64,1,3]{0,1,3,2:T(8,128)} %fusion.666) | copy-start | bytes 147460
  550.1 7.7 %copy-start.81 = (f32[64,64,1,3]{0,1,3,2:T(8,128)S(1)}, f32[64,64,1,3]{0,1,3,2:T(8,128)}, u32[]{:S(2)}) copy-start(f32[64,64,1,3]{0,1,3,2:T(8,128)} %fusion.664) | copy-start | bytes 147460
  550.2 7.7 %copy-start.82 = (f32[64,64,1,3]{0,1,3,2:T(8,128)S(1)}, f32[64,64,1,3]{0,1,3,2:T(8,128)}, u32[]{:S(2)}) copy-start(f32[64,64,1,3]{0,1,3,2:T(8,128)} %fusion.662) | copy-start | bytes 147460
  553.8 158.8 %all-to-all-start.5 = ((bf16[16,2,4096]{2,1,0:T(2,128)(2,1)}), bf16[16,2,4096]{2,1,0:T(2,128)(2,1)S(1)}, u32[]{:S(2)}, u32[]{:S(2)}) async-start(bf16[16,2,4096]{2,1,0:T(2,128)(2,1)} %reshape.843), calls=%async_computation.5 | async-start | bytes 524288 | tf_op jit(solution)/shard_map/all_to_all | solution.py:181
  557.8 152.1 %all-reduce.28.cloned.1.call-start = ((), (), s32[]{:S(2)}) async-start(), calls=%async_computation.6 | async-start | bytes 1179648 | tf_op jit(solution)/shard_map/psum | solution.py:182
  (144 other events, 379.8 us)
Sparse Core Ops, SparseCore 0:
  564.0 145.8 all-reduce.27
where the time goes:
time: 733 us; the launch traced here: 721 us
  local copies, waits for them, and re-layouts  215 us (29%)
  waiting for transfers between devices  162 us (22%)
  matrix products  159 us (22%)
  blocking collectives  63.5 us (9%)
  other arithmetic  47.4 us (6%)
  between operations  39.2 us (5%)
  starting transfers between devices  34.7 us (5%)
    psum x1, waiting for transfers between devices, per_device(): lax.psum((raw_weight_h, raw_weight_v, raw_beta_h, raw_beta_v), ('vrow', '...  150 us
    transpose x30, matrix products, conv_weight(): return jnp.transpose(result, (1, 0, 2, 3))  84.4 us
    unnamed x371, local copies, waits for them, and re-layouts  75.8 us
    psum x1, blocking collectives, per_device(): lax.psum((raw_weight_h, raw_weight_v, raw_beta_h, raw_beta_v), ('vrow', '...  63.5 us
    conv_general_dilated x30, matrix products, conv_taps(): lax.conv_general_dilated(source, kernel_row, (1, 1), ((0, 0), (0, 0)), di...  52.2 us
    dynamic_slice x38, local copies, waits for them, and re-layouts, window(): return lax.dynamic_slice(padded, starts, sizes)  44.9 us
    mul x15, local copies, waits for them, and re-layouts, masked_source(): return (extended * inside[None, None].astype(extended.dtype), inside)  38 us
    conv_general_dilated x30, matrix products, conv_back(): lax.conv_general_dilated(grads, kernel_row, (1, 1), ((0, 0), (0, 0)), dim...  22 us
  transfers between devices with their start and end apart: 7, of which 4 were waited for; matrix products, arithmetic and copies ran while one was open for 6% of the time, Pallas kernels for 0%

commit v1 on v0

--- a/solution.py
+++ b/solution.py
@@ -180,7 +180,7 @@
     ).reshape(u_local, y_local, x_all, v_all * channels)
     grad_features = lax.all_to_all(dhor_stored, "img", split_axis=2, concat_axis=1, tiled=True)
     raw_weight_h, raw_weight_v, raw_beta_h, raw_beta_v = lax.psum(
-        (raw_weight_h, raw_weight_v, raw_beta_h, raw_beta_v), ("vrow", "img")
+        lax.psum((raw_weight_h, raw_weight_v, raw_beta_h, raw_beta_v), "vrow"), "img"
     )
     factor = float(u_all * v_all * y_all * x_all) ** (-0.5)
     return (

time: 733 us -> 711 us (0.970)
  the two profiles are of different devices: /device:TPU:1 before, /device:TPU:0 now
where the time goes in v1:
time: 711 us; the launch traced here: 699 us
  local copies, waits for them, and re-layouts  213 us (30%)
  matrix products  159 us (22%)
  waiting for transfers between devices  155 us (22%)
  blocking collectives  52.4 us (7%)
  other arithmetic  48.3 us (7%)
  between operations  39.9 us (6%)
  starting transfers between devices  31.3 us (4%)
    psum x1, waiting for transfers between devices, per_device(): lax.psum(lax.psum((raw_weight_h, raw_weight_v, raw_beta_h, raw_beta_v), '...  117 us
    transpose x30, matrix products, conv_weight(): return jnp.transpose(result, (1, 0, 2, 3))  85.1 us
    unnamed x349, local copies, waits for them, and re-layouts  74.4 us
    conv_general_dilated x30, matrix products, conv_taps(): lax.conv_general_dilated(source, kernel_row, (1, 1), ((0, 0), (0, 0)), di...  52.3 us
    dynamic_slice x38, local copies, waits for them, and re-layouts, window(): return lax.dynamic_slice(padded, starts, sizes)  44.9 us
    mul x15, local copies, waits for them, and re-layouts, masked_source(): return (extended * inside[None, None].astype(extended.dtype), inside)  38.3 us
    psum x1, blocking collectives, per_device(): lax.psum(lax.psum((raw_weight_h, raw_weight_v, raw_beta_h, raw_beta_v), '...  28.6 us
    psum x1, waiting for transfers between devices, per_device(): lax.psum((raw_weight_h, raw_weight_v, raw_beta_h, raw_beta_v), 'vrow')  24.8 us
  transfers between devices with their start and end apart: 8, of which 5 were waited for; matrix products, arithmetic and copies ran while one was open for 7% of the time, Pallas kernels for 0%

profile of v1, /device:TPU:0, one launch (start us, length us, event | category | flops | bytes accessed | tf_op | source)
XLA Modules:
  0.0 699.0 jit_solution(1191617104975017040)
XLA Ops:
  7.2 5.5 all-to-all-start
  37.4 15.5 %broadcast_multiply_fusion.4 = (bf16[1,64,16,134]{1,0,3,2:T(2,128)(2,1)S(1)}, bf16[1,64,16,134]{1,0,3,2:T(2,128)(2,1)S(1)}, bf16[1,64,16,134]{1,0,3,2:T(2,128)(2...) fusion(bf16[16,134]{1,0:T(8,128)(2,1)S(1)} %copy-done.110, bf16[1,64,16,128]{1,0,3,2:T(2,128)(2,1)S(1)} %copy.364, ...), kind=kLoop, calls=%fused_computation.390 | loop fusion | flops 686080 | bytes 1655744 | tf_op jit(solution)/shard_map/mul | solution.py:61
  132.0 6.5 pad_dynamic-slice_fusion.35
  166.3 6.7 pad_dynamic-slice_fusion.31
  216.3 7.6 %all-to-all-start.1 = ((bf16[1,1,64,16,128]{4,2,1,0,3:T(8,128)(2,1)}), bf16[1,1,64,16,128]{4,2,1,0,3:T(8,128)(2,1)S(1)}, u32[]{:S(2)}, u32[]{:S(2)}) async-start(bf16[1,1,64,16,128]{4,2,1,0,3:T(8,128)(2,1)} %copy.435), calls=%async_computation.1 | async-start | bytes 524288 | tf_op jit(solution)/shard_map/all_to_all | solution.py:141
  224.6 8.7 %all-to-all-done.1 = bf16[1,1,64,16,128]{4,2,1,0,3:T(8,128)(2,1)S(1)} async-done(((bf16[1,1,64,16,128]{4,2,1,0,3:T(8,128)(2,1)}), bf16[1,1,64,16,128]{4,2,1,0,3:T(8,128)(2,1)S(1)}, u32[]{:S(2)}, u32[]{:S(2)}) %all-to-all-start.1) | async-done | bytes 262176 | tf_op jit(solution)/shard_map/all_to_all | solution.py:141
  235.3 5.0 all-to-all-start.2
  321.2 5.7 fusion.86
  333.3 5.4 all-to-all-start.4
  358.5 4.5 fusion.666
  363.0 4.5 fusion.664
  368.8 4.4 fusion.662
  373.2 4.5 fusion.663
  377.7 4.5 fusion.661
  387.8 4.5 fusion.660
  392.4 4.5 fusion.658
  402.5 4.5 fusion.657
  407.0 4.5 fusion.655
  417.1 4.5 fusion.654
  421.6 4.5 fusion.652
  493.1 23.8 %all-reduce.26 = (f32[5,64]{1,0:T(8,128)S(1)}, f32[5,64]{1,0:T(8,128)S(1)}) all-reduce(f32[5,64]{1,0:T(8,128)S(1)} %stack.89, f32[5,64]{1,0:T(8,128)S(1)} %copy-done.115), channel_id=1, replica_groups=mesh['vrow'=8,'img'=16] {'vrow'}, use_global_device_ids=true, to_apply=%region_9.10 | all-reduce | flops 640 | bytes 5120 | tf_op jit(solution)/shard_map/psum | solution.py:183
  516.9 28.6 %all-reduce.24 = (f32[5,64]{1,0:T(8,128)S(1)}, f32[5,64]{1,0:T(8,128)S(1)}) all-reduce(f32[5,64]{1,0:T(8,128)S(1)} %get-tuple-element.44, f32[5,64]{1,0:T(8,128)S(1)} %get-tuple-element.45), channel_id=1, replica_groups=mesh['vrow'=8,'img'=16] {'img'}, use_global_device_ids=true, to_apply=%region_10.11 | all-reduce | flops 640 | bytes 5120 | tf_op jit(solution)/shard_map/psum | solution.py:182
  545.5 24.8 %all-reduce.33.cloned.1.call-done = (f32[64,64,3,3]{0,1,3,2:T(8,128)}, f32[64,64,3,3]{0,1,3,2:T(8,128)}) async-done(((f32[64,64,3,3]{0,1,3,2:T(8,128)}, f32[64,64,3,3]{0,1,3,2:T(8,128)}), (f32[64,64,3,3]{0,1,3,2:T(8,128)}, f32[64,64,3,3]{0,1,3,2:T(8,128)})) %all-reduce.33.cloned.1.call-update) | async-done | bytes 294928 | tf_op jit(solution)/shard_map/psum | solution.py:183
  572.6 116.6 %all-reduce.31.cloned.1.call-done = (f32[64,64,3,3]{0,1,3,2:T(8,128)}, f32[64,64,3,3]{0,1,3,2:T(8,128)}) async-done(((f32[64,64,3,3]{0,1,3,2:T(8,128)}, f32[64,64,3,3]{0,1,3,2:T(8,128)}), (f32[64,64,3,3]{0,1,3,2:T(8,128)}, f32[64,64,3,3]{0,1,3,2:T(8,128)})) %all-reduce.31.cloned.1.call-update) | async-done | bytes 294928 | tf_op jit(solution)/shard_map/psum | solution.py:182
  (651 shorter events, 349.2 us)
Async XLA Ops:
  7.2 28.2 %all-to-all-start = ((bf16[1,16,8,1024]{3,2,0,1:T(8,128)(2,1)}), bf16[1,16,8,1024]{3,2,0,1:T(8,128)(2,1)S(1)}, u32[]{:S(2)}, u32[]{:S(2)}) async-start(bf16[1,16,8,1024]{3,2,0,1:T(8,128)(2,1)} %bitcast.649), calls=%async_computation | async-start | bytes 524288 | tf_op jit(solution)/shard_map/all_to_all | solution.py:132
  52.9 56.5 %copy-start.3 = (bf16[1,64,16,134]{1,0,3,2:T(2,128)(2,1)}, bf16[1,64,16,134]{1,0,3,2:T(2,128)(2,1)S(1)}, u32[]{:S(2)}) copy-start(bf16[1,64,16,134]{1,0,3,2:T(2,128)(2,1)S(1)} %get-tuple-element.104) | copy-start | bytes 823300
  52.9 79.1 %copy-start.5 = (bf16[1,64,16,134]{1,0,3,2:T(2,128)(2,1)}, bf16[1,64,16,134]{1,0,3,2:T(2,128)(2,1)S(1)}, u32[]{:S(2)}) copy-start(bf16[1,64,16,134]{1,0,3,2:T(2,128)(2,1)S(1)} %get-tuple-element.105) | copy-start | bytes 823300
  52.9 79.1 %copy-start.7 = (bf16[1,64,16,134]{1,0,3,2:T(2,128)(2,1)}, bf16[1,64,16,134]{1,0,3,2:T(2,128)(2,1)S(1)}, u32[]{:S(2)}) copy-start(bf16[1,64,16,134]{1,0,3,2:T(2,128)(2,1)S(1)} %get-tuple-element.106) | copy-start | bytes 823300
  132.0 81.9 %copy-start.12 = (f32[16,1,128,64]{2,0,3,1:T(8,128)}, f32[16,1,128,64]{2,0,3,1:T(8,128)S(1)}, u32[]{:S(2)}) copy-start(f32[16,1,128,64]{2,0,3,1:T(8,128)S(1)} %copy.541) | copy-start | bytes 1572868
  158.7 55.2 %copy-start.14 = (f32[16,1,128,64]{2,0,3,1:T(8,128)}, f32[16,1,128,64]{2,0,3,1:T(8,128)S(1)}, u32[]{:S(2)}) copy-start(f32[16,1,128,64]{2,0,3,1:T(8,128)S(1)} %copy.542) | copy-start | bytes 1572868
  206.1 7.8 %copy-start.18 = (f32[16,1,128,64]{2,0,3,1:T(8,128)}, f32[16,1,128,64]{2,0,3,1:T(8,128)S(1)}, u32[]{:S(2)}) copy-start(f32[16,1,128,64]{2,0,3,1:T(8,128)S(1)} %copy.544) | copy-start | bytes 1572868
  214.0 9.9 %copy-start.142 = (f32[5,64]{1,0:T(8,128)S(1)}, f32[5,64]{1,0:T(8,128)}, u32[]{:S(2)}) copy-start(f32[5,64]{1,0:T(8,128)} %param.11) | copy-start | bytes 3844
  214.0 10.5 %copy-start.129 = (pred[8,22]{1,0:T(8,128)(4,1)S(1)}, pred[8,22]{1,0:T(8,128)(4,1)}, u32[]{:S(2)}) copy-start(pred[8,22]{1,0:T(8,128)(4,1)} %get-tuple-element.145) | copy-start | bytes 532
  214.0 10.5 %copy-start.130 = (pred[8,22]{1,0:T(8,128)(4,1)S(1)}, pred[8,22]{1,0:T(8,128)(4,1)}, u32[]{:S(2)}) copy-start(pred[8,22]{1,0:T(8,128)(4,1)} %get-tuple-element.168) | copy-start | bytes 532
  216.3 17.0 %all-to-all-start.1 = ((bf16[1,1,64,16,128]{4,2,1,0,3:T(8,128)(2,1)}), bf16[1,1,64,16,128]{4,2,1,0,3:T(8,128)(2,1)S(1)}, u32[]{:S(2)}, u32[]{:S(2)}) async-start(bf16[1,1,64,16,128]{4,2,1,0,3:T(8,128)(2,1)} %copy.435), calls=%async_computation.1 | async-start | bytes 524288 | tf_op jit(solution)/shard_map/all_to_all | solution.py:141
  224.5 47.6 %copy-start.131 = (f32[64]{0:T(128)}, f32[64]{0:T(128)S(1)}, u32[]{:S(2)}) copy-start(f32[64]{0:T(128)S(1)} %get-tuple-element.130) | copy-start | bytes 772
  233.8 6.5 copy-start.128
  235.2 19.5 %copy-start.126 = (pred[8,22]{1,0:T(8,128)(4,1)S(1)}, pred[8,22]{1,0:T(8,128)(4,1)}, u32[]{:S(2)}) copy-start(pred[8,22]{1,0:T(8,128)(4,1)} %get-tuple-element.164) | copy-start | bytes 532
  235.2 19.5 %copy-start.127 = (pred[8,22]{1,0:T(8,128)(4,1)S(1)}, pred[8,22]{1,0:T(8,128)(4,1)}, u32[]{:S(2)}) copy-start(pred[8,22]{1,0:T(8,128)(4,1)} %get-tuple-element.166) | copy-start | bytes 532
  235.2 19.6 %copy-start.50 = (f32[16,8,17,64]{3,1,2,0:T(8,128)S(1)}, f32[16,8,17,64]{3,1,2,0:T(8,128)}, u32[]{:S(2)}) copy-start(f32[16,8,17,64]{3,1,2,0:T(8,128)} %get-tuple-element.92) | copy-start | bytes 1671172
  235.3 32.7 %all-to-all-start.2 = ((bf16[16,2,4096]{2,1,0:T(2,128)(2,1)}), bf16[16,2,4096]{2,1,0:T(2,128)(2,1)}, u32[]{:S(2)}, u32[]{:S(2)}) async-start(bf16[16,2,4096]{2,1,0:T(2,128)(2,1)} %reshape.837), calls=%async_computation.2 | async-start | bytes 524288 | tf_op jit(solution)/shard_map/all_to_all | solution.py:140
  317.1 13.7 %all-to-all-start.3 = ((bf16[8,2,8192]{2,1,0:T(2,128)(2,1)}), bf16[8,2,8192]{2,1,0:T(2,128)(2,1)}, u32[]{:S(2)}, u32[]{:S(2)}) async-start(bf16[8,2,8192]{2,1,0:T(2,128)(2,1)} %reshape.839), calls=%async_computation.3 | async-start | bytes 524288 | tf_op jit(solution)/shard_map/all_to_all | solution.py:168
  332.1 6.6 copy-start.149
  333.3 13.1 %all-to-all-start.4 = ((bf16[16,2,4096]{2,1,0:T(2,128)(2,1)}), bf16[16,2,4096]{2,1,0:T(2,128)(2,1)S(1)}, u32[]{:S(2)}, u32[]{:S(2)}) async-start(bf16[16,2,4096]{2,1,0:T(2,128)(2,1)} %reshape.841), calls=%async_computation.4 | async-start | bytes 524288 | tf_op jit(solution)/shard_map/all_to_all | solution.py:167
  338.7 231.6 %all-reduce.33.cloned.1.call-start = ((), (), s32[]{:S(2)}) async-start(), calls=%async_computation.7 | async-start | bytes 1179648 | tf_op jit(solution)/shard_map/psum | solution.py:183
  486.0 7.2 %copy-start.115 = (f32[5,64]{1,0:T(8,128)S(1)}, f32[5,64]{1,0:T(8,128)}, u32[]{:S(2)}) copy-start(f32[5,64]{1,0:T(8,128)} %stack.95) | copy-start | bytes 3844
  489.5 82.0 %all-to-all-start.5 = ((bf16[16,2,4096]{2,1,0:T(2,128)(2,1)}), bf16[16,2,4096]{2,1,0:T(2,128)(2,1)S(1)}, u32[]{:S(2)}, u32[]{:S(2)}) async-start(bf16[16,2,4096]{2,1,0:T(2,128)(2,1)} %reshape.843), calls=%async_computation.5 | async-start | bytes 524288 | tf_op jit(solution)/shard_map/all_to_all | solution.py:181
  493.1 196.1 %all-reduce.31.cloned.1.call-start = ((), (), s32[]{:S(2)}) async-start(), calls=%async_computation.6 | async-start | bytes 1179648 | tf_op jit(solution)/shard_map/psum | solution.py:182
  (134 other events, 274.8 us)
Sparse Core Ops, SparseCore 0:
  482.8 87.4 all-reduce.32
  572.9 116.2 all-reduce.30
